TPU v7x, 32 devices: a whole 2x2x4 slice. The times are simulated.
32 devices in a mesh: wide: 4 (over z), narrow: 8 (over y, x, core).
Axes of the slice: x: 2, y: 2, z: 4, core: 2. Of those that a mesh axis runs over, the one named last changes fastest.
Arguments:
- src_design: float32 [5, 4194304], P(None, ('wide', 'narrow')), may hold values from -6 to 6
- att_design: float32 [16, 4194304], P(None, ('wide', 'narrow')), may hold values from -3 to 3
- right_side: float32 [4194304], P(('wide', 'narrow')), may hold values from -6 to 6
- block_source: int32 [65536], P(('wide', 'narrow')), may hold values from 0 to 65535, as said below
- block_segment: int32 [65536], P(('wide', 'narrow')), may hold values from 0 to 8191, as said below
- block_count: int32 [65536], P(('wide', 'narrow')), may hold values from 8 to 64
Outputs:
- sol_src: float32 [5, 65536], P(None, ('wide', 'narrow'))
- sol_att: float32 [16, 8192], P(None, 'narrow')
- dir_src: float32 [5, 65536], P(None, ('wide', 'narrow'))
- dir_att: float32 [16, 8192], P(None, 'narrow')
Inputs may be any that keep to these rules, and one draw needn't show every extreme that they name: `block_source`: A block held by the device at index w of wide names a source in [w * 2048 * 8, (w + 1) * 2048 * 8); of the 2048 blocks of one device, exactly 2048 / 8 name sources in [(w * 8 + m) * 2048, (w * 8 + m + 1) * 2048) for each m in 0 to 8 - 1; the lowest and highest source of the partition are named on every device. `block_segment`: A block held by the device at index n of narrow names a segment in [n * 1024, (n + 1) * 1024); the lowest and highest of that range are named on every device.
All inputs are finite; a program needn't handle non-finite values.
Results may differ from a plain program's by a relative error of at most 0.00018.
Values sent between devices are 32-bit elements; how exact they have to be, the bound alone decides.
No kernel may reach another device: no remote copies, remote signals or barrier semaphores. Data moves between devices by JAX's collectives and lax.ppermute only.
A program may use at most 192 MiB of HBM per device.

v0:
```python
import jax
import jax.numpy as jnp
from jax import lax
from jax.sharding import PartitionSpec as P

ITERS = 2
SRC_DEV = 2048
SEG_DEV = 1024


def on_device(src_design, att_design, right_side, block_source, block_segment, block_count):
    block_total = block_source.shape[0]
    narrow_size = lax.axis_size("narrow")
    group_size = SRC_DEV * narrow_size
    wide_at = lax.axis_index("wide")
    narrow_at = lax.axis_index("narrow")
    src_index = block_source - wide_at * group_size
    seg_index = block_segment - narrow_at * SEG_DEV
    src_blocks = src_design.reshape(src_design.shape[0], block_total, -1)
    att_blocks = att_design.reshape(att_design.shape[0], block_total, -1)
    param_rows = src_blocks.shape[0]
    obs_width = src_blocks.shape[2]
    live_rows = (jnp.arange(obs_width, dtype=jnp.int32)[None, :] < block_count[:, None]).astype(
        jnp.float32
    )
    att_weight = (wide_at == 0).astype(jnp.float32)
    src_weight = jnp.float32(1.0)

    def transposed(obs_vec):
        src_part = jnp.sum(src_blocks * obs_vec[None], axis=2)
        att_part = jnp.sum(att_blocks * obs_vec[None], axis=2)
        att_total = (
            jnp.zeros((att_blocks.shape[0], SEG_DEV), jnp.float32).at[:, seg_index].add(att_part)
        )
        att_vec = lax.psum(att_total, "wide")
        src_total = jnp.zeros((param_rows, group_size), jnp.float32).at[:, src_index].add(src_part)
        src_vec = lax.psum_scatter(src_total, "narrow", scatter_dimension=1, tiled=True)
        return (src_vec, att_vec)

    def param_dot(first_src, first_att, second_src, second_att):
        return src_weight * jnp.sum(first_src * second_src) + att_weight * jnp.sum(
            first_att * second_att
        )

    def merged_total(first, second, third, fourth):
        return lax.psum((first, second, third, fourth), ("wide", "narrow"))

    obs_vec = right_side.reshape(block_total, obs_width) * live_rows
    src_raw, att_raw = transposed(obs_vec)
    zero_val = jnp.float32(0.0)
    totals = merged_total(
        jnp.sum(obs_vec * obs_vec),
        param_dot(src_raw, att_raw, src_raw, att_raw),
        zero_val,
        zero_val,
    )
    beta_norm = jnp.sqrt(totals[0])
    alpha_norm = jnp.sqrt(totals[1]) / beta_norm
    obs_vec = obs_vec / beta_norm
    src_vec = src_raw / beta_norm / alpha_norm
    att_vec = att_raw / beta_norm / alpha_norm
    dir_src, dir_att = (src_vec, att_vec)
    sol_src = jnp.zeros_like(src_vec)
    sol_att = jnp.zeros_like(att_vec)
    phi_bar = beta_norm
    rho_bar = alpha_norm
    for step in range(ITERS):
        whole_src = lax.all_gather(src_vec, "narrow", axis=1, tiled=True)
        src_vals = jnp.take(whole_src, src_index, axis=1)
        att_vals = jnp.take(att_vec, seg_index, axis=1)
        image = jnp.sum(src_blocks * src_vals[:, :, None], axis=0)
        image = image + jnp.sum(att_blocks * att_vals[:, :, None], axis=0)
        obs_raw = image * live_rows - alpha_norm * obs_vec
        src_raw, att_raw = transposed(obs_raw)
        totals = merged_total(
            jnp.sum(obs_raw * obs_raw),
            param_dot(src_raw, att_raw, src_raw, att_raw),
            param_dot(src_raw, att_raw, src_vec, att_vec),
            param_dot(src_vec, att_vec, src_vec, att_vec),
        )
        beta_norm = jnp.sqrt(totals[0])
        alpha_square = (
            totals[1] / (beta_norm * beta_norm)
            - 2.0 * totals[2]
            + beta_norm * beta_norm * totals[3]
        )
        alpha_norm = jnp.sqrt(alpha_square)
        obs_vec = obs_raw / beta_norm
        src_vec = (src_raw / beta_norm - beta_norm * src_vec) / alpha_norm
        att_vec = (att_raw / beta_norm - beta_norm * att_vec) / alpha_norm
        rho_val = jnp.sqrt(rho_bar * rho_bar + beta_norm * beta_norm)
        cosine = rho_bar / rho_val
        sine_part = beta_norm / rho_val
        theta_val = sine_part * alpha_norm
        rho_bar = -cosine * alpha_norm
        phi_val = cosine * phi_bar
        phi_bar = sine_part * phi_bar
        sol_src = sol_src + phi_val / rho_val * dir_src
        sol_att = sol_att + phi_val / rho_val * dir_att
        dir_src = src_vec - theta_val / rho_val * dir_src
        dir_att = att_vec - theta_val / rho_val * dir_att
    return (sol_src, sol_att, dir_src, dir_att)


def solution(mesh):
    in_specs = (
        P(None, ("wide", "narrow")),
        P(None, ("wide", "narrow")),
        P(("wide", "narrow")),
        P(("wide", "narrow")),
        P(("wide", "narrow")),
        P(("wide", "narrow")),
    )
    out_specs = (
        P(None, ("wide", "narrow")),
        P(None, "narrow"),
        P(None, ("wide", "narrow")),
        P(None, "narrow"),
    )
    return jax.shard_map(
        on_device, mesh=mesh, in_specs=in_specs, out_specs=out_specs, check_vma=False
    )
```

profile of v0, /device:TPU:0, one launch (start us, length us, event | category | flops | bytes accessed | tf_op | source)
XLA Modules:
  0.0 607.7 jit_solution(5175881611888121235)
XLA Ops:
  8.1 17.4 %reshape.145 = f32[16,2048,64]{2,1,0:T(8,128)} reshape(f32[16,131072]{1,0:T(8,128)} %param.11) | data formatting | bytes 16777216 | tf_op jit(solution)/shard_map/reshape | solution.py:20
  26.1 8.2 %multiply_reduce_fusion.2 = f32[16,2048]{1,0:T(8,128)S(1)} fusion(f32[16,2048,64]{2,1,0:T(8,128)} %reshape.145, f32[2048,64]{1,0:T(8,128)S(1)} %fusion.6), kind=kLoop, calls=%fused_computation.12 | loop fusion | flops 4161536 | bytes 9043968 | tf_op jit(solution)/shard_map/reduce_sum | solution.py:31
  35.7 12.0 %scatter_custom_fusion.1 = f32[16,1024]{0,1:T(8,128)S(1)} fusion(s32[2048]{0:T(1024)S(1)} %get-tuple-element.45, f32[2048,16]{1,0:T(8,128)} %copy.42, f32[]{:T(128)} %constant.27.clone.1), kind=kCustom, calls=%fused_computation.43 | custom fusion | flops 32768 | bytes 66048 | tf_op jit(solution)/shard_map/scatter-add | solution.py:33
  59.7 15.2 %scatter_custom_fusion = f32[5,16384]{0,1:T(8,128)} fusion(s32[2048]{0:T(1024)S(1)} %get-tuple-element.47, f32[2048,5]{1,0:T(8,128)S(1)} %copy.40, f32[]{:T(128)} %constant.27.clone.1), kind=kCustom, calls=%fused_computation.24 | custom fusion | flops 10240 | bytes 327684 | tf_op jit(solution)/shard_map/scatter-add | solution.py:36
  87.8 30.0 %reduce-scatter.4.cloned.1.call-done = f32[5,2048]{1,0:T(8,128)} async-done(((f32[5,16384]{1,0:T(8,128)}), f32[5,2048]{1,0:T(8,128)}) %reduce-scatter.4.cloned.1.call-update) | async-done | bytes 40976 | tf_op jit(solution)/shard_map/reduce_scatter | solution.py:37
  119.9 39.6 %all-reduce.2 = (f32[]{:T(128)}, f32[]{:T(128)}) all-reduce(f32[]{:T(128)} %multiply_reduce_fusion.12, f32[]{:T(128)S(6)} %add.133), channel_id=1, replica_groups=mesh['wide'=4,'narrow'=8] {'wide','narrow'}, use_global_device_ids=true, to_apply=%region_10.0 | all-reduce | flops 2 | bytes 16 | tf_op jit(solution)/shard_map/psum | solution.py:46
  161.7 10.8 %all_gather.6 = f32[5,16384]{1,0:T(8,128)S(1)} all-gather(f32[5,2048]{1,0:T(8,128)S(1)} %broadcast_divide_fusion.1), channel_id=1, replica_groups=mesh['wide'=4,'narrow'=8] {'narrow'}, dimensions={1}, use_global_device_ids=true | all-gather | bytes 368640 | tf_op jit(solution)/shard_map/all_gather | solution.py:68
  178.2 11.0 %gather_fusion = f32[2048,5]{1,0:T(8,128)} fusion(f32[5,16384]{0,1:T(8,128)} %copy.44, s32[2048]{0:T(1024)S(1)} %broadcast_clamp_fusion.1), kind=kCustom, calls=%fused_computation.clone | custom fusion | bytes 90112 | tf_op jit(solution)/shard_map/jit(_take)/gather | solution.py:69
  216.1 8.3 %mul.348 = f32[16,2048,64]{2,1,0:T(8,128)} broadcast(f32[16,2048]{1,0:T(8,128)S(1)} %copy.47), dimensions={0,1} | broadcast | bytes 8519680 | tf_op jit(solution)/shard_map/mul | solution.py:72
  224.4 15.5 %mul.349 = f32[16,131072]{1,0:T(8,128)} reshape(f32[16,2048,64]{2,1,0:T(8,128)} %mul.348) | data formatting | bytes 16777216 | tf_op jit(solution)/shard_map/mul | solution.py:72
  251.1 8.4 %multiply_reduce_fusion.1 = f32[16,2048]{1,0:T(8,128)S(1)} fusion(f32[16,2048,64]{2,1,0:T(8,128)} %reshape.145, f32[2048,64]{1,0:T(8,128)S(1)} %multiply_subtract_fusion.1), kind=kLoop, calls=%fused_computation.11 | loop fusion | flops 4161536 | bytes 9043968 | tf_op jit(solution)/shard_map/reduce_sum | solution.py:31
  260.8 12.0 %scatter_custom_fusion.3 = f32[16,1024]{0,1:T(8,128)S(1)} fusion(s32[2048]{0:T(1024)S(1)} %get-tuple-element.45, f32[2048,16]{1,0:T(8,128)} %copy.50, f32[]{:T(128)} %constant.27.clone.1), kind=kCustom, calls=%fused_computation.41 | custom fusion | flops 32768 | bytes 66048 | tf_op jit(solution)/shard_map/scatter-add | solution.py:33
  278.0 15.2 %scatter_custom_fusion.2 = f32[5,16384]{0,1:T(8,128)} fusion(s32[2048]{0:T(1024)S(1)} %get-tuple-element.47, f32[2048,5]{1,0:T(8,128)S(1)} %copy.48, f32[]{:T(128)} %constant.27.clone.1), kind=kCustom, calls=%fused_computation.22 | custom fusion | flops 10240 | bytes 327684 | tf_op jit(solution)/shard_map/scatter-add | solution.py:36
  310.5 21.9 %reduce-scatter.6.cloned.1.call-done = f32[5,2048]{1,0:T(8,128)} async-done(((f32[5,16384]{1,0:T(8,128)}), f32[5,2048]{1,0:T(8,128)}) %reduce-scatter.6.cloned.1.call-update) | async-done | bytes 40976 | tf_op jit(solution)/shard_map/reduce_scatter | solution.py:37
  335.9 39.6 %all-reduce.1 = (f32[]{:T(128)}, f32[]{:T(128)}, f32[]{:T(128)}, f32[]{:T(128)}) all-reduce(f32[]{:T(128)S(6)} %add.137, f32[]{:T(128)} %get-tuple-element.42, f32[]{:T(128)S(6)} %add.138, f32[]{:T(128)S(6)} %add.139), channel_id=1, replica_groups=mesh['wide'=4,'narrow'=8] {'wide','narrow'}, use_global_device_ids=true, to_apply=%region_23.26 | all-reduce | flops 4 | bytes 32 | tf_op jit(solution)/shard_map/psum | solution.py:46
  389.2 9.2 %mul.384 = f32[16,2048,64]{2,1,0:T(8,128)} broadcast(f32[16,2048]{1,0:T(8,128)} %copy.55), dimensions={0,1} | broadcast | bytes 8519680 | tf_op jit(solution)/shard_map/mul | solution.py:72
  398.4 15.5 %mul.385 = f32[16,131072]{1,0:T(8,128)} reshape(f32[16,2048,64]{2,1,0:T(8,128)} %mul.384) | data formatting | bytes 16777216 | tf_op jit(solution)/shard_map/mul | solution.py:72
  413.9 8.2 %multiply_reduce_fusion.3 = f32[131072]{0:T(1024)} fusion(f32[16,131072]{1,0:T(8,128)} %param.11, f32[16,131072]{1,0:T(8,128)} %mul.385), kind=kLoop, calls=%fused_computation.13 | loop fusion | flops 4063232 | bytes 17301504 | tf_op jit(solution)/shard_map/reduce_sum | solution.py:72
  422.1 10.9 %all_gather.7 = f32[5,16384]{1,0:T(8,128)S(1)} all-gather(f32[5,2048]{1,0:T(8,128)S(1)} %subtract_divide_fusion.1), channel_id=1, replica_groups=mesh['wide'=4,'narrow'=8] {'narrow'}, dimensions={1}, use_global_device_ids=true | all-gather | bytes 368640 | tf_op jit(solution)/shard_map/all_gather | solution.py:68
  438.5 11.0 %gather_fusion.2 = f32[2048,5]{1,0:T(8,128)} fusion(f32[5,16384]{0,1:T(8,128)} %copy.52, s32[2048]{0:T(1024)S(1)} %broadcast_clamp_fusion.1), kind=kCustom, calls=%fused_computation.2.clone | custom fusion | bytes 90112 | tf_op jit(solution)/shard_map/jit(_take)/gather | solution.py:69
  479.3 11.7 %scatter_custom_fusion.5 = f32[16,1024]{0,1:T(8,128)S(1)} fusion(s32[2048]{0:T(1024)} %copy-done.7, f32[2048,16]{1,0:T(8,128)S(1)} %copy.58, f32[]{:T(128)} %constant.27.clone.1), kind=kCustom, calls=%fused_computation.39 | custom fusion | flops 32768 | bytes 66048 | tf_op jit(solution)/shard_map/scatter-add | solution.py:33
  496.2 15.6 %scatter_custom_fusion.4 = f32[5,16384]{0,1:T(8,128)} fusion(s32[2048]{0:T(1024)} %copy-done.8, f32[2048,5]{1,0:T(8,128)S(1)} %copy.56, f32[]{:T(128)} %constant.27.clone.1), kind=kCustom, calls=%fused_computation.20 | custom fusion | flops 10240 | bytes 328192 | tf_op jit(solution)/shard_map/scatter-add | solution.py:36
  528.8 22.3 %reduce-scatter.8.cloned.1.call-done = f32[5,2048]{1,0:T(8,128)} async-done(((f32[5,16384]{1,0:T(8,128)}), f32[5,2048]{1,0:T(8,128)}) %reduce-scatter.8.cloned.1.call-update) | async-done | bytes 40976 | tf_op jit(solution)/shard_map/reduce_scatter | solution.py:37
  554.5 39.6 %all-reduce = (f32[]{:T(128)}, f32[]{:T(128)}, f32[]{:T(128)}, f32[]{:T(128)}) all-reduce(f32[]{:T(128)} %get-tuple-element.40, f32[]{:T(128)S(6)} %add.146, f32[]{:T(128)S(6)} %add.147, f32[]{:T(128)S(6)} %add.148), channel_id=1, replica_groups=mesh['wide'=4,'narrow'=8] {'wide','narrow'}, use_global_device_ids=true, to_apply=%region_33.36 | all-reduce | flops 4 | bytes 32 | tf_op jit(solution)/shard_map/psum | solution.py:46
  (104 shorter events, 166.7 us)
Async XLA Ops:
  8.0 77.6 %all-reduce.7.cloned.1.call-start = ((), (), s32[]{:S(2)}) async-start(), calls=%async_computation.4 | async-start | bytes 131072 | tf_op jit(solution)/shard_map/psum | solution.py:35
  8.0 17.4 %copy-start = (f32[131072]{0:T(1024)S(1)}, f32[131072]{0:T(1024)}, u32[]{:S(2)}) copy-start(f32[131072]{0:T(1024)} %param.12) | copy-start | bytes 1572868
  8.1 17.6 %copy-start.6 = (s32[2048]{0:T(1024)S(1)}, s32[2048]{0:T(1024)}, u32[]{:S(2)}) copy-start(s32[2048]{0:T(1024)} %param.15) | copy-start | bytes 24580
  26.0 9.6 %copy-start.10 = (s32[2048]{0:T(1024)S(1)}, s32[2048]{0:T(1024)}, u32[]{:S(2)}) copy-start(s32[2048]{0:T(1024)} %param.14) | copy-start | bytes 24580
  35.6 225.2 %copy-start.7 = (s32[2048]{0:T(1024)}, s32[2048]{0:T(1024)S(1)}, u32[]{:S(2)}) copy-start(s32[2048]{0:T(1024)S(1)} %get-tuple-element.45) | copy-start | bytes 24580
  35.7 23.6 %copy-start.11 = (s32[2048]{0:T(1024)S(1)}, s32[2048]{0:T(1024)}, u32[]{:S(2)}) copy-start(s32[2048]{0:T(1024)} %param.13) | copy-start | bytes 24580
  48.5 69.3 %reduce-scatter.4.cloned.1.call-start = ((), (), s32[]{:S(2)}) async-start(), calls=%async_computation.3 | async-start | bytes 589824 | tf_op jit(solution)/shard_map/reduce_scatter | solution.py:37
  59.3 129.9 %copy-start.9 = (pred[2048]{0:T(1024)(128)(4,1)}, pred[2048]{0:T(1024)(128)(4,1)S(1)}, u32[]{:S(2)}) copy-start(pred[2048]{0:T(1024)(128)(4,1)S(1)} %get-tuple-element.46) | copy-start | bytes 6148
  59.3 218.7 %copy-start.8 = (s32[2048]{0:T(1024)}, s32[2048]{0:T(1024)S(1)}, u32[]{:S(2)}) copy-start(s32[2048]{0:T(1024)S(1)} %get-tuple-element.47) | copy-start | bytes 24580
  80.9 226.2 %all-reduce.9.cloned.1.call-start = ((), (), s32[]{:S(2)}) async-start(), calls=%async_computation.6 | async-start | bytes 131072 | tf_op jit(solution)/shard_map/psum | solution.py:35
  194.5 11.9 %copy-start.3 = (f32[16,1024]{1,0:T(8,128)S(1)}, f32[16,1024]{1,0:T(8,128)}, u32[]{:S(2)}) copy-start(f32[16,1024]{1,0:T(8,128)} %all-reduce.7.cloned.1.call-done) | copy-start | bytes 196612
  239.9 7.6 %copy-start.1 = (f32[131072]{0:T(1024)S(1)}, f32[131072]{0:T(1024)}, u32[]{:S(2)}) copy-start(f32[131072]{0:T(1024)} %multiply_reduce_fusion.9) | copy-start | bytes 1572868
  273.6 58.8 %reduce-scatter.6.cloned.1.call-start = ((), (), s32[]{:S(2)}) async-start(), calls=%async_computation.5 | async-start | bytes 589824 | tf_op jit(solution)/shard_map/reduce_scatter | solution.py:37
  278.0 54.5 %copy-start.4 = (f32[5,2048]{1,0:T(8,128)S(1)}, f32[5,2048]{1,0:T(8,128)}, u32[]{:S(2)}) copy-start(f32[5,2048]{1,0:T(8,128)} %reduce-scatter.4.cloned.1.call-done) | copy-start | bytes 122884
  299.2 226.2 %all-reduce.11.cloned.1.call-start = ((), (), s32[]{:S(2)}) async-start(), calls=%async_computation.8 | async-start | bytes 131072 | tf_op jit(solution)/shard_map/psum | solution.py:35
  413.9 8.2 %copy-start.5 = (f32[5,2048]{1,0:T(8,128)S(1)}, f32[5,2048]{1,0:T(8,128)}, u32[]{:S(2)}) copy-start(f32[5,2048]{1,0:T(8,128)} %reduce-scatter.6.cloned.1.call-done) | copy-start | bytes 122884
  456.1 11.2 %copy-start.2 = (f32[131072]{0:T(1024)S(1)}, f32[131072]{0:T(1024)}, u32[]{:S(2)}) copy-start(f32[131072]{0:T(1024)} %multiply_reduce_fusion.3) | copy-start | bytes 1572868
  491.8 59.2 %reduce-scatter.8.cloned.1.call-start = ((), (), s32[]{:S(2)}) async-start(), calls=%async_computation.7 | async-start | bytes 589824 | tf_op jit(solution)/shard_map/reduce_scatter | solution.py:37
Sparse Core Ops, SparseCore 0:
  48.6 37.0 all-reduce.6
  273.7 33.3 all-reduce.8
  492.0 33.3 all-reduce.10
Sparse Core Ops, SparseCore 1:
  81.0 36.8 reduce-scatter.3
  299.3 33.1 reduce-scatter.5
  517.8 33.1 reduce-scatter.7
where the time goes:
time: 616 us; the launch traced here: 608 us
  local copies, waits for them, and re-layouts  171 us (28%)
  other arithmetic  171 us (28%)
  blocking collectives  140 us (23%)
  waiting for transfers between devices  92.8 us (15%)
  between operations  32.3 us (5%)
    psum x3, blocking collectives, merged_total(): return lax.psum((first, second, third, fourth), ('wide', 'narrow'))  119 us
    reduce_scatter x3, waiting for transfers between devices, transposed(): lax.psum_scatter(src_total, 'narrow', scatter_dimension=1, tiled=True)  74.2 us
    mul x4, local copies, waits for them, and re-layouts, on_device(): image = image + jnp.sum(att_blocks * att_vals[:, :, None], axis=0)  48.4 us
    scatter-add x3, other arithmetic, transposed(): jnp.zeros((param_rows, group_size), jnp.float32).at[:, src_index]  45.9 us
    scatter-add x3, other arithmetic, transposed(): jnp.zeros((att_blocks.shape[0], SEG_DEV), jnp.float32).at[:, seg_index]  35.6 us
    reduce_sum x3, other arithmetic, transposed(): att_part = jnp.sum(att_blocks * obs_vec[None], axis=2)  24.9 us
    gather x2, local copies, waits for them, and re-layouts, on_device(): src_vals = jnp.take(whole_src, src_index, axis=1)  21.9 us
    all_gather x2, blocking collectives, on_device(): whole_src = lax.all_gather(src_vec, 'narrow', axis=1, tiled=True)  21.7 us
  transfers between devices with their start and end apart: 6, of which 6 were waited for; matrix products, arithmetic and copies ran while one was open for 15% of the time, Pallas kernels for 0%

commit v1 on v0

--- a/solution.py
+++ b/solution.py
@@ -6,6 +6,24 @@
 ITERS = 2
 SRC_DEV = 2048
 SEG_DEV = 1024
+
+
+def in_order(blocks, dim):
+    blocks = jnp.moveaxis(blocks, 0, dim)
+    shape = blocks.shape
+    return blocks.reshape(*shape[:dim], shape[dim] * shape[dim + 1], *shape[dim + 2 :])
+
+
+def grow_blocks(x, axis):
+    size = lax.axis_size(axis)
+    tiles = x[None]
+    for level in range(size.bit_length() - 1):
+        bit = 1 << level
+        other = lax.ppermute(tiles, axis, [(i, i ^ bit) for i in range(size)])
+        both = jnp.stack([tiles, other])
+        upper = lax.axis_index(axis) >> level & 1
+        tiles = jnp.where(upper == 0, both, both[::-1]).reshape(-1, *x.shape)
+    return tiles
 
 
 def on_device(src_design, att_design, right_side, block_source, block_segment, block_count):
@@ -65,7 +83,7 @@
     phi_bar = beta_norm
     rho_bar = alpha_norm
     for step in range(ITERS):
-        whole_src = lax.all_gather(src_vec, "narrow", axis=1, tiled=True)
+        whole_src = in_order(grow_blocks(src_vec, "narrow"), 1)
         src_vals = jnp.take(whole_src, src_index, axis=1)
         att_vals = jnp.take(att_vec, seg_index, axis=1)
         image = jnp.sum(src_blocks * src_vals[:, :, None], axis=0)

time: 616 us -> 728 us (1.18)
  waiting for transfers between devices: 92.8 us -> 202 us
  blocking collectives: 140 us -> 119 us
  other arithmetic: 171 us -> 184 us
  starting transfers between devices: 0.46 us -> 8.9 us
    reduce_scatter x3, waiting for transfers between devices: 74.2 us -> 168 us  [transposed(): lax.psum_scatter(src_total, 'narrow', scatter_dimension=1, tiled=True)]
    all_gather x2 -> x0, blocking collectives: 21.7 us -> none  [on_device(): whole_src = lax.all_gather(src_vec, 'narrow', axis=1, tiled=True)]
    scatter-add x3 -> x0, local copies, waits for them, and re-layouts: 18 us -> none  [transposed(): jnp.zeros((param_rows, group_size), jnp.float32).at[:, src_index]]
    psum x3, waiting for transfers between devices: 18.5 us -> 34.5 us  [transposed(): att_vec = lax.psum(att_total, 'wide')]
    all_gather x2 -> x0, local copies, waits for them, and re-layouts: 11.2 us -> none  [on_device(): whole_src = lax.all_gather(src_vec, 'narrow', axis=1, tiled=True)]
    transpose x0 -> x2, local copies, waits for them, and re-layouts: none -> 10.5 us  [in_order(): blocks = jnp.moveaxis(blocks, 0, dim)]
    ppermute x0 -> x6, starting transfers between devices: none -> 8.22 us  [grow_blocks(): other = lax.ppermute(tiles, axis, [(i, i ^ bit) for i in range(size)])]
  transfers between devices with their start and end apart: 6 -> 12, of which waited for: 6 -> 6; matrix products, arithmetic and copies ran while one was open for 15% -> 22% of each run, Pallas kernels for 0% -> 0%
where the time goes in v1:
time: 728 us; the launch traced here: 720 us
  waiting for transfers between devices  202 us (28%)
  other arithmetic  184 us (25%)
  local copies, waits for them, and re-layouts  172 us (24%)
  blocking collectives  119 us (16%)
  between operations  32.7 us (4%)
  starting transfers between devices  8.9 us (1%)
    reduce_scatter x3, waiting for transfers between devices, transposed(): lax.psum_scatter(src_total, 'narrow', scatter_dimension=1, tiled=True)  168 us
    psum x3, blocking collectives, merged_total(): return lax.psum((first, second, third, fourth), ('wide', 'narrow'))  119 us
    mul x4, local copies, waits for them, and re-layouts, on_device(): image = image + jnp.sum(att_blocks * att_vals[:, :, None], axis=0)  47.6 us
    scatter-add x3, other arithmetic, transposed(): jnp.zeros((param_rows, group_size), jnp.float32).at[:, src_index]  45.6 us
    scatter-add x3, other arithmetic, transposed(): jnp.zeros((att_blocks.shape[0], SEG_DEV), jnp.float32).at[:, seg_index]  35.5 us
    psum x3, waiting for transfers between devices, transposed(): att_vec = lax.psum(att_total, 'wide')  34.5 us
    reduce_sum x3, other arithmetic, transposed(): att_part = jnp.sum(att_blocks * obs_vec[None], axis=2)  25.1 us
    gather x2, local copies, waits for them, and re-layouts, on_device(): src_vals = jnp.take(whole_src, src_index, axis=1)  21.9 us
  transfers between devices with their start and end apart: 12, of which 6 were waited for; matrix products, arithmetic and copies ran while one was open for 22% of the time, Pallas kernels for 0%

profile of v1, /device:TPU:0, one launch (start us, length us, event | category | flops | bytes accessed | tf_op | source)
XLA Modules:
  0.0 719.7 jit_solution(10501464689899645234)
XLA Ops:
  8.1 17.4 %reshape.169 = f32[16,2048,64]{2,1,0:T(8,128)} reshape(f32[16,131072]{1,0:T(8,128)} %param.11) | data formatting | bytes 16777216 | tf_op jit(solution)/shard_map/reshape | solution.py:38
  35.7 12.0 %scatter_custom_fusion.1 = f32[16,1024]{0,1:T(8,128)S(1)} fusion(s32[2048]{0:T(1024)S(1)} %get-tuple-element.53, f32[2048,16]{1,0:T(8,128)} %copy.75, f32[]{:T(128)} %constant.27.clone.1), kind=kCustom, calls=%fused_computation.59 | custom fusion | flops 32768 | bytes 66048 | tf_op jit(solution)/shard_map/scatter-add | solution.py:51
  59.7 15.2 %scatter_custom_fusion = f32[5,16384]{0,1:T(8,128)} fusion(s32[2048]{0:T(1024)S(1)} %get-tuple-element.55, f32[2048,5]{1,0:T(8,128)S(1)} %copy.74, f32[]{:T(128)} %constant.27.clone.1), kind=kCustom, calls=%fused_computation.24 | custom fusion | flops 10240 | bytes 327684 | tf_op jit(solution)/shard_map/scatter-add | solution.py:54
  76.3 9.3 %all-reduce.7.cloned.1.call-done = f32[16,1024]{1,0:T(8,128)} async-done(((f32[16,1024]{1,0:T(8,128)}), f32[16,1024]{1,0:T(8,128)}) %all-reduce.7.cloned.1.call-update) | async-done | bytes 65552 | tf_op jit(solution)/shard_map/psum | solution.py:53
  87.8 61.2 %reduce-scatter.4.cloned.1.call-done = f32[5,2048]{0,1:T(8,128)} async-done(((f32[5,16384]{0,1:T(8,128)}), f32[5,2048]{0,1:T(8,128)}) %reduce-scatter.4.cloned.1.call-update) | async-done | bytes 40976 | tf_op jit(solution)/shard_map/reduce_scatter | solution.py:55
  151.8 40.0 %all-reduce.2 = (f32[]{:T(128)}, f32[]{:T(128)}) all-reduce(f32[]{:T(128)} %multiply_reduce_fusion.19, f32[]{:T(128)S(6)} %add.133), channel_id=1, replica_groups=mesh['wide'=4,'narrow'=8] {'wide','narrow'}, use_global_device_ids=true, to_apply=%region_10.0 | all-reduce | flops 2 | bytes 16 | tf_op jit(solution)/shard_map/psum | solution.py:64
  211.1 8.3 %mul.348 = f32[16,2048,64]{2,1,0:T(8,128)} broadcast(f32[16,2048]{1,0:T(8,128)S(1)} %copy.85), dimensions={0,1} | broadcast | bytes 8519680 | tf_op jit(solution)/shard_map/mul | solution.py:90
  219.4 15.5 %mul.349 = f32[16,131072]{1,0:T(8,128)} reshape(f32[16,2048,64]{2,1,0:T(8,128)} %mul.348) | data formatting | bytes 16777216 | tf_op jit(solution)/shard_map/mul | solution.py:90
  249.6 11.0 %gather_fusion = f32[2048,5]{1,0:T(8,128)} fusion(f32[5,16384]{0,1:T(8,128)} %bitcast.53, s32[2048]{0:T(1024)S(1)} %broadcast_clamp_fusion.1), kind=kCustom, calls=%fused_computation.clone | custom fusion | bytes 90112 | tf_op jit(solution)/shard_map/jit(_take)/gather | solution.py:87
  289.3 11.6 %scatter_custom_fusion.3 = f32[16,1024]{0,1:T(8,128)S(1)} fusion(s32[2048]{0:T(1024)S(1)} %get-tuple-element.53, f32[2048,16]{1,0:T(8,128)S(1)} %copy.87, f32[]{:T(128)} %constant.27.clone.1), kind=kCustom, calls=%fused_computation.57 | custom fusion | flops 32768 | bytes 65540 | tf_op jit(solution)/shard_map/scatter-add | solution.py:51
  306.1 15.2 %scatter_custom_fusion.2 = f32[5,16384]{0,1:T(8,128)} fusion(s32[2048]{0:T(1024)S(1)} %get-tuple-element.55, f32[2048,5]{1,0:T(8,128)S(1)} %copy.86, f32[]{:T(128)} %constant.27.clone.1), kind=kCustom, calls=%fused_computation.22 | custom fusion | flops 10240 | bytes 327684 | tf_op jit(solution)/shard_map/scatter-add | solution.py:54
  321.6 12.8 %all-reduce.9.cloned.1.call-done = f32[16,1024]{1,0:T(8,128)} async-done(((f32[16,1024]{1,0:T(8,128)}), f32[16,1024]{1,0:T(8,128)}) %all-reduce.9.cloned.1.call-update) | async-done | bytes 65552 | tf_op jit(solution)/shard_map/psum | solution.py:53
  337.8 53.1 %reduce-scatter.6.cloned.1.call-done = f32[5,2048]{0,1:T(8,128)} async-done(((f32[5,16384]{0,1:T(8,128)}), f32[5,2048]{0,1:T(8,128)}) %reduce-scatter.6.cloned.1.call-update) | async-done | bytes 40976 | tf_op jit(solution)/shard_map/reduce_scatter | solution.py:55
  395.1 39.6 %all-reduce.1 = (f32[]{:T(128)}, f32[]{:T(128)}, f32[]{:T(128)}, f32[]{:T(128)}) all-reduce(f32[]{:T(128)S(6)} %add.137, f32[]{:T(128)} %get-tuple-element.50, f32[]{:T(128)S(6)} %add.138, f32[]{:T(128)S(6)} %add.139), channel_id=1, replica_groups=mesh['wide'=4,'narrow'=8] {'wide','narrow'}, use_global_device_ids=true, to_apply=%region_23.26 | all-reduce | flops 4 | bytes 32 | tf_op jit(solution)/shard_map/psum | solution.py:64
  441.0 8.6 %gather_fusion.3 = f32[2048,16]{1,0:T(8,128)} fusion(f32[16,1024]{0,1:T(8,128)} %copy.96, s32[2048]{0:T(1024)S(1)} %broadcast_clamp_fusion), kind=kCustom, calls=%fused_computation.3.clone | custom fusion | bytes 270336 | tf_op jit(solution)/shard_map/jit(_take)/gather | solution.py:88
  464.9 8.3 %mul.384 = f32[16,2048,64]{2,1,0:T(8,128)} broadcast(f32[16,2048]{1,0:T(8,128)S(1)} %copy.97), dimensions={0,1} | broadcast | bytes 8519680 | tf_op jit(solution)/shard_map/mul | solution.py:90
  473.3 15.5 %mul.385 = f32[16,131072]{1,0:T(8,128)} reshape(f32[16,2048,64]{2,1,0:T(8,128)} %mul.384) | data formatting | bytes 16777216 | tf_op jit(solution)/shard_map/mul | solution.py:90
  511.0 11.0 %gather_fusion.2 = f32[2048,5]{1,0:T(8,128)} fusion(f32[5,16384]{0,1:T(8,128)} %bitcast.52, s32[2048]{0:T(1024)S(1)} %broadcast_clamp_fusion.1), kind=kCustom, calls=%fused_computation.2.clone | custom fusion | bytes 90112 | tf_op jit(solution)/shard_map/jit(_take)/gather | solution.py:87
  546.7 8.6 %multiply_reduce_fusion = f32[16,2048]{1,0:T(8,128)S(1)} fusion(f32[16,2048,64]{2,1,0:T(8,128)} %reshape.169, f32[2048,64]{1,0:T(8,128)S(1)} %multiply_subtract_fusion.1), kind=kLoop, calls=%fused_computation.10 | loop fusion | flops 4161536 | bytes 9043968 | tf_op jit(solution)/shard_map/reduce_sum | solution.py:49
  556.6 11.9 %scatter_custom_fusion.5 = f32[16,1024]{0,1:T(8,128)S(1)} fusion(s32[2048]{0:T(1024)} %copy-done.14, f32[2048,16]{1,0:T(8,128)} %copy.99, f32[]{:T(128)} %constant.27.clone.1), kind=kCustom, calls=%fused_computation.55 | custom fusion | flops 32768 | bytes 66048 | tf_op jit(solution)/shard_map/scatter-add | solution.py:51
  574.0 15.3 %scatter_custom_fusion.4 = f32[5,16384]{0,1:T(8,128)} fusion(s32[2048]{0:T(1024)} %copy-done.15, f32[2048,5]{1,0:T(8,128)S(1)} %copy.98, f32[]{:T(128)} %constant.27.clone.1), kind=kCustom, calls=%fused_computation.20 | custom fusion | flops 10240 | bytes 328192 | tf_op jit(solution)/shard_map/scatter-add | solution.py:54
  589.6 12.4 %all-reduce.11.cloned.1.call-done = f32[16,1024]{1,0:T(8,128)} async-done(((f32[16,1024]{1,0:T(8,128)}), f32[16,1024]{1,0:T(8,128)}) %all-reduce.11.cloned.1.call-update) | async-done | bytes 65552 | tf_op jit(solution)/shard_map/psum | solution.py:53
  605.4 53.5 %reduce-scatter.8.cloned.1.call-done = f32[5,2048]{0,1:T(8,128)} async-done(((f32[5,16384]{0,1:T(8,128)}), f32[5,2048]{0,1:T(8,128)}) %reduce-scatter.8.cloned.1.call-update) | async-done | bytes 40976 | tf_op jit(solution)/shard_map/reduce_scatter | solution.py:55
  663.0 39.6 %all-reduce = (f32[]{:T(128)}, f32[]{:T(128)}, f32[]{:T(128)}, f32[]{:T(128)}) all-reduce(f32[]{:T(128)} %get-tuple-element.48, f32[]{:T(128)S(6)} %add.146, f32[]{:T(128)S(6)} %add.147, f32[]{:T(128)S(6)} %add.148), channel_id=1, replica_groups=mesh['wide'=4,'narrow'=8] {'wide','narrow'}, use_global_device_ids=true, to_apply=%region_33.36 | all-reduce | flops 4 | bytes 32 | tf_op jit(solution)/shard_map/psum | solution.py:64
  (157 shorter events, 180.3 us)
Async XLA Ops:
  8.0 77.6 %all-reduce.7.cloned.1.call-start = ((), (), s32[]{:S(2)}) async-start(), calls=%async_computation.4 | async-start | bytes 131072 | tf_op jit(solution)/shard_map/psum | solution.py:53
  8.0 17.4 %copy-start.2 = (f32[131072]{0:T(1024)S(1)}, f32[131072]{0:T(1024)}, u32[]{:S(2)}) copy-start(f32[131072]{0:T(1024)} %param.12) | copy-start | bytes 1572868
  8.1 17.6 %copy-start.13 = (s32[2048]{0:T(1024)S(1)}, s32[2048]{0:T(1024)}, u32[]{:S(2)}) copy-start(s32[2048]{0:T(1024)} %param.15) | copy-start | bytes 24580
  35.7 253.6 %copy-start.14 = (s32[2048]{0:T(1024)}, s32[2048]{0:T(1024)S(1)}, u32[]{:S(2)}) copy-start(s32[2048]{0:T(1024)S(1)} %get-tuple-element.53) | copy-start | bytes 24580
  35.7 23.6 %copy-start.19 = (s32[2048]{0:T(1024)S(1)}, s32[2048]{0:T(1024)}, u32[]{:S(2)}) copy-start(s32[2048]{0:T(1024)} %param.13) | copy-start | bytes 24580
  48.5 100.5 %reduce-scatter.4.cloned.1.call-start = ((), (), s32[]{:S(2)}) async-start(), calls=%async_computation.3 | async-start | bytes 9437184 | tf_op jit(solution)/shard_map/reduce_scatter | solution.py:55
  59.3 201.3 %copy-start.16 = (pred[2048]{0:T(1024)(128)(4,1)}, pred[2048]{0:T(1024)(128)(4,1)S(1)}, u32[]{:S(2)}) copy-start(pred[2048]{0:T(1024)(128)(4,1)S(1)} %get-tuple-element.54) | copy-start | bytes 6148
  59.3 246.8 %copy-start.15 = (s32[2048]{0:T(1024)}, s32[2048]{0:T(1024)S(1)}, u32[]{:S(2)}) copy-start(s32[2048]{0:T(1024)S(1)} %get-tuple-element.55) | copy-start | bytes 24580
  74.9 259.5 %all-reduce.9.cloned.1.call-start = ((), (), s32[]{:S(2)}) async-start(), calls=%async_computation.6 | async-start | bytes 131072 | tf_op jit(solution)/shard_map/psum | solution.py:53
  197.1 9.0 %collective-permute-start = (f32[1,5,2048]{2,0,1:T(1,128)S(1)}, f32[1,5,2048]{2,0,1:T(1,128)S(1)}, u32[]{:S(2)}, u32[]{:S(2)}) collective-permute-start(f32[1,5,2048]{2,0,1:T(1,128)S(1)} %copy.77), channel_id=1, source_target_pairs={{0,1},{1,0},{2,3},{3,2},{4,5},{5,4},{6,7},{7,6},{8,9},{9,8},{10,11... | collective-permute-start | bytes 122888 | tf_op jit(solution)/shard_map/ppermute | solution.py:22
  206.9 28.0 %collective-permute-start.1 = (f32[2,5,2048]{2,0,1:T(2,128)S(1)}, f32[2,5,2048]{2,0,1:T(2,128)S(1)}, u32[]{:S(2)}, u32[]{:S(2)}) collective-permute-start(f32[2,5,2048]{2,0,1:T(2,128)S(1)} %get-tuple-element.63), channel_id=1, source_target_pairs={{0,2},{1,3},{2,0},{3,1},{4,6},{5,7},{6,4},{7,5},{8,10},{9,11},{10,... | collective-permute-start | bytes 245768 | tf_op jit(solution)/shard_map/ppermute | solution.py:22
  235.3 9.4 %collective-permute-start.2 = (f32[4,5,2048]{2,0,1:T(4,128)S(1)}, f32[4,5,2048]{2,0,1:T(4,128)S(1)}, u32[]{:S(2)}, u32[]{:S(2)}) collective-permute-start(f32[4,5,2048]{2,0,1:T(4,128)S(1)} %reshape.171), channel_id=1, source_target_pairs={{0,4},{1,5},{2,6},{3,7},{4,0},{5,1},{6,2},{7,3},{8,12},{9,13},{10,... | collective-permute-start | bytes 491528 | tf_op jit(solution)/shard_map/ppermute | solution.py:22
  301.7 89.2 %reduce-scatter.6.cloned.1.call-start = ((), (), s32[]{:S(2)}) async-start(), calls=%async_computation.5 | async-start | bytes 9437184 | tf_op jit(solution)/shard_map/reduce_scatter | solution.py:55
  306.1 28.3 %copy-start.7 = (f32[16,1024]{1,0:T(8,128)S(1)}, f32[16,1024]{1,0:T(8,128)}, u32[]{:S(2)}) copy-start(f32[16,1024]{1,0:T(8,128)} %all-reduce.7.cloned.1.call-done) | copy-start | bytes 196612
  306.1 84.8 %copy-start = (f32[5,2048]{0,1:T(8,128)S(1)}, f32[5,2048]{0,1:T(8,128)}, u32[]{:S(2)}) copy-start(f32[5,2048]{0,1:T(8,128)} %reduce-scatter.4.cloned.1.call-done) | copy-start | bytes 122884
  321.3 280.6 %all-reduce.11.cloned.1.call-start = ((), (), s32[]{:S(2)}) async-start(), calls=%async_computation.8 | async-start | bytes 131072 | tf_op jit(solution)/shard_map/psum | solution.py:53
  439.0 10.9 %collective-permute-start.3 = (f32[1,5,2048]{2,0,1:T(1,128)S(1)}, f32[1,5,2048]{2,0,1:T(1,128)S(1)}, u32[]{:S(2)}, u32[]{:S(2)}) collective-permute-start(f32[1,5,2048]{2,0,1:T(1,128)S(1)} %copy.89), channel_id=1, source_target_pairs={{0,1},{1,0},{2,3},{3,2},{4,5},{5,4},{6,7},{7,6},{8,9},{9,8},{10,11... | collective-permute-start | bytes 122888 | tf_op jit(solution)/shard_map/ppermute | solution.py:22
  439.9 33.3 %copy-start.8 = (f32[16,1024]{1,0:T(8,128)}, f32[16,1024]{1,0:T(8,128)S(1)}, u32[]{:S(2)}) copy-start(f32[16,1024]{1,0:T(8,128)S(1)} %subtract_divide_fusion.1) | copy-start | bytes 196612
  458.6 30.2 %collective-permute-start.4 = (f32[2,5,2048]{2,0,1:T(2,128)}, f32[2,5,2048]{2,0,1:T(2,128)}, u32[]{:S(2)}, u32[]{:S(2)}) collective-permute-start(f32[2,5,2048]{2,0,1:T(2,128)} %get-tuple-element.61), channel_id=1, source_target_pairs={{0,2},{1,3},{2,0},{3,1},{4,6},{5,7},{6,4},{7,5},{8,10},{9,11},{10,... | collective-permute-start | bytes 245768 | tf_op jit(solution)/shard_map/ppermute | solution.py:22
  490.6 10.8 %collective-permute-start.5 = (f32[4,5,2048]{2,0,1:T(4,128)}, f32[4,5,2048]{2,0,1:T(4,128)}, u32[]{:S(2)}, u32[]{:S(2)}) collective-permute-start(f32[4,5,2048]{2,0,1:T(4,128)} %reshape.175), channel_id=1, source_target_pairs={{0,4},{1,5},{2,6},{3,7},{4,0},{5,1},{6,2},{7,3},{8,12},{9,13},{10,... | collective-permute-start | bytes 491528 | tf_op jit(solution)/shard_map/ppermute | solution.py:22
  500.6 21.3 %copy-start.17 = (pred[2048]{0:T(1024)(128)(4,1)S(1)}, pred[2048]{0:T(1024)(128)(4,1)}, u32[]{:S(2)}) copy-start(pred[2048]{0:T(1024)(128)(4,1)} %copy-done.16) | copy-start | bytes 6148
  569.4 89.5 %reduce-scatter.8.cloned.1.call-start = ((), (), s32[]{:S(2)}) async-start(), calls=%async_computation.7 | async-start | bytes 9437184 | tf_op jit(solution)/shard_map/reduce_scatter | solution.py:55
  574.0 27.9 %copy-start.9 = (f32[16,1024]{1,0:T(8,128)S(1)}, f32[16,1024]{1,0:T(8,128)}, u32[]{:S(2)}) copy-start(f32[16,1024]{1,0:T(8,128)} %copy-done.8) | copy-start | bytes 196612
  601.9 109.4 %copy-start.11 = (f32[16,1024]{1,0:T(8,128)S(1)}, f32[16,1024]{1,0:T(8,128)}, u32[]{:S(2)}) copy-start(f32[16,1024]{1,0:T(8,128)} %all-reduce.11.cloned.1.call-done) | copy-start | bytes 196612
  (8 other events, 61.1 us)
Sparse Core Ops, SparseCore 0:
  48.6 37.0 all-reduce.6
  301.9 32.4 all-reduce.8
  569.5 32.3 all-reduce.10
Sparse Core Ops, SparseCore 1:
  74.9 74.0 reduce-scatter.3
  321.4 69.5 reduce-scatter.5
  589.4 69.4 reduce-scatter.7
